TPU v7x, 512 devices: a whole 4x8x8 slice. The times are simulated.
512 devices in a mesh: tok: 16 (over z, core), voc: 32 (over y, x).
Axes of the slice: x: 4, y: 8, z: 8, core: 2. Of those that a mesh axis runs over, the one named last changes fastest.
Arguments:
- hidden: bfloat16 [256, 2304], P('tok', 'voc'), may hold values from -18 to 18
- head: bfloat16 [2304, 131072], P(None, ('tok', 'voc')), as said below
- targets: int32 [256], replicated, may hold values from 0 to 131071
- probe_hidden: bfloat16 [256, 2304], P('tok', 'voc'), may hold values from -6 to 6
- probe_head: bfloat16 [2304, 131072], P(None, ('tok', 'voc')), may hold values from -0.5 to 0.5
Outputs:
- head_out: float32 [2304, 131072], P(None, ('tok', 'voc'))
- hidden_out: float32 [256, 2304], P('tok', 'voc')
Inputs may be any that keep to these rules, and one draw needn't show every extreme that they name: `head`: entries lie within 66 / sqrt(2304) in magnitude.
All inputs are finite; a program needn't handle non-finite values.
Results may differ from a plain program's by a relative error of at most 0.0075.
Values may be sent and summed in bfloat16 or wider, within the bound.
A program may use at most 64 MiB of HBM per device.

v0:
```python
import jax
import jax.numpy as jnp
from jax import lax
from jax.sharding import PartitionSpec as P

softcap_value = 30.0
zloss_weight = 0.0001


def local(hidden, head, targets, probe_hidden, probe_head):
    voc_count = lax.axis_size("voc")
    vocab_width = head.shape[1]
    stacked = jnp.stack([hidden, probe_hidden])
    features = lax.all_gather(stacked, "voc", axis=2, tiled=True)
    gathered = lax.all_gather(features, "tok", axis=1, tiled=True)
    row_hidden = gathered[0]
    row_probe = gathered[1]
    logits = jnp.dot(row_hidden, head, preferred_element_type=jnp.float32)
    tangent = jnp.dot(row_probe, head, preferred_element_type=jnp.float32) + jnp.dot(
        row_hidden, probe_head, preferred_element_type=jnp.float32
    )
    capped = jnp.tanh(logits / softcap_value)
    cap_slope = 1.0 - capped * capped
    exponent = jnp.exp(softcap_value * capped)
    cap_tangent = cap_slope * tangent
    row_total = lax.psum(jnp.sum(exponent, axis=1), ("tok", "voc"))
    probability = exponent / row_total[:, None]
    mean_tangent = lax.psum(jnp.sum(probability * cap_tangent, axis=1), ("tok", "voc"))
    factor = 1.0 + 2.0 * zloss_weight * jnp.log(row_total)
    offset = (lax.axis_index("tok") * voc_count + lax.axis_index("voc")) * vocab_width
    columns = offset + lax.iota(jnp.int32, vocab_width)
    onehot = (targets[:, None] == columns[None, :]).astype(jnp.float32)
    grad_cap = factor[:, None] * probability - onehot
    grad_tan = probability * (
        factor[:, None] * (cap_tangent - mean_tangent[:, None])
        + 2.0 * zloss_weight * mean_tangent[:, None]
    )
    slope_tan = -2.0 / softcap_value * capped * cap_slope * tangent
    dlogit = (grad_cap * cap_slope).astype(jnp.bfloat16)
    dlogit_tan = (grad_tan * cap_slope + grad_cap * slope_tan).astype(jnp.bfloat16)
    head_out = jnp.einsum(
        "krd,krv->dv", gathered, jnp.stack([dlogit_tan, dlogit]), preferred_element_type=jnp.float32
    )
    probe_part = lax.dot_general(
        dlogit, probe_head, (((1,), (1,)), ((), ())), preferred_element_type=jnp.float32
    )
    head_part = lax.dot_general(
        dlogit_tan, head, (((1,), (1,)), ((), ())), preferred_element_type=jnp.float32
    )
    summed = lax.psum_scatter(probe_part + head_part, "tok", scatter_dimension=0, tiled=True)
    hidden_out = lax.psum_scatter(summed, "voc", scatter_dimension=1, tiled=True)
    return (head_out, hidden_out)


def solution(mesh):
    return jax.shard_map(
        local,
        mesh=mesh,
        in_specs=(
            P("tok", "voc"),
            P(None, ("tok", "voc")),
            P(),
            P("tok", "voc"),
            P(None, ("tok", "voc")),
        ),
        out_specs=(P(None, ("tok", "voc")), P("tok", "voc")),
        check_vma=False,
    )
```

profile of v0, /device:TPU:2, one launch (start us, length us, event | category | flops | bytes accessed | tf_op | source)
XLA Modules:
  0.0 533.8 jit_solution(17602048826722212761)
XLA Ops:
  7.2 0.0 copy-start
  7.2 0.0 all-gather.2.cloned.1.call-start
  7.2 0.8 pad_maximum_fusion
  8.0 0.1 copy.12
  8.1 52.7 %all_gather.6 = bf16[2,16,2304]{1,0,2:T(2,128)(2,1)S(1)} all-gather(bf16[2,16,72]{1,0,2:T(2,128)(2,1)S(1)} %copy.12), channel_id=1, replica_groups=mesh['tok'=16,'voc'=32] {'voc'}, dimensions={2}, use_global_device_ids=true | all-gather | bytes 152064 | tf_op jit(solution)/shard_map/all_gather | solution.py:14
  60.8 2.2 copy.13
  63.0 0.0 all-gather.2.cloned.1.call-update
  63.0 0.0 reduce-scatter.3.cloned.1.call-start
  63.1 0.6 iota_add_fusion
  63.7 42.7 %all-gather.2.cloned.1.call-done = bf16[2,256,2304]{2,1,0:T(8,128)(2,1)} async-done(((bf16[2,16,2304]{2,1,0:T(8,128)(2,1)}), bf16[2,256,2304]{2,1,0:T(8,128)(2,1)}) %all-gather.2.cloned.1.call-update) | async-done | bytes 2359312 | tf_op jit(solution)/shard_map/all_gather | solution.py:15
  106.4 0.0 copy-done
  106.4 2.7 fusion.8
  109.1 96.8 %psum.14 = f32[256]{0:T(256)S(1)} all-reduce(f32[256]{0:T(256)S(1)} %get-tuple-element.4), channel_id=1, replica_groups=mesh['tok'=16,'voc'=32] {'tok','voc'}, use_global_device_ids=true, to_apply=%region_1.0 | all-reduce | flops 256 | bytes 2048 | tf_op jit(solution)/shard_map/psum | solution.py:26
  205.8 0.0 copy-done.1
  205.8 0.0 copy-start.4
  205.8 1.9 fusion.3
  207.7 0.0 copy-done.4
  207.8 0.0 copy-start.5
  207.8 1.8 multiply_reduce_fusion
  209.6 94.9 %psum.15 = f32[256]{0:T(256)S(1)} all-reduce(f32[256]{0:T(256)} %get-tuple-element.6), channel_id=1, replica_groups=mesh['tok'=16,'voc'=32] {'tok','voc'}, use_global_device_ids=true, to_apply=%region_3.0 | all-reduce | flops 256 | bytes 2048 | tf_op jit(solution)/shard_map/psum | solution.py:28
  304.5 0.0 copy-done.5
  304.5 1.2 add_convert_fusion
  305.8 1.9 fusion.10
  307.7 2.0 convolution_add_fusion
  309.6 0.0 reduce-scatter.3.cloned.1.call-update
  309.7 0.0 all-reduce.3.cloned.1.call-start
  309.7 1.3 dynamic-slice
  311.6 58.5 %reduce-scatter.3.cloned.1.call-done = f32[16,2304]{1,0:T(8,128)} async-done(((f32[256,2304]{1,0:T(8,128)}), f32[16,2304]{1,0:T(8,128)}) %reduce-scatter.3.cloned.1.call-update) | async-done | bytes 147472 | tf_op jit(solution)/shard_map/reduce_scatter | solution.py:50
  370.1 0.0 all-reduce.3.cloned.1.call-update
  370.1 3.2 convolution_bitcast_fusion
  373.3 152.5 %all-reduce.3.cloned.1.call-done = f32[16,2304]{1,0:T(8,128)} async-done(((f32[16,2304]{1,0:T(8,128)}), f32[16,2304]{1,0:T(8,128)}) %all-reduce.3.cloned.1.call-update) | async-done | bytes 147472
  525.9 1.4 constant_dynamic-slice_fusion
  (7 shorter events, 0.0 us)
Async XLA Ops:
  7.2 99.2 %copy-start = (bf16[2304,256]{1,0:T(8,128)(2,1)S(1)}, bf16[2304,256]{1,0:T(8,128)(2,1)}, u32[]{:S(2)}) copy-start(bf16[2304,256]{1,0:T(8,128)(2,1)} %param.6) | copy-start | bytes 3538948
  7.2 99.2 %all-gather.2.cloned.1.call-start = ((), (), s32[]{:S(2)}) async-start(), calls=%async_computation.1 | async-start | bytes 2506752 | tf_op jit(solution)/shard_map/all_gather | solution.py:15
  63.0 307.1 %reduce-scatter.3.cloned.1.call-start = ((), (), s32[]{:S(2)}) async-start(), calls=%async_computation.2 | async-start | bytes 2506752 | tf_op jit(solution)/shard_map/reduce_scatter | solution.py:50
  106.4 99.5 %copy-start.1 = (bf16[2,256,2304]{2,1,0:T(8,128)(2,1)S(1)}, bf16[2,256,2304]{2,1,0:T(8,128)(2,1)}, u32[]{:S(2)}) copy-start(bf16[2,256,2304]{2,1,0:T(8,128)(2,1)} %all-gather.2.cloned.1.call-done) | copy-start | bytes 7077892
  205.8 1.9 copy-start.4
  207.8 96.8 %copy-start.5 = (s32[256]{0:T(256)S(1)}, s32[256]{0:T(256)}, u32[]{:S(2)}) copy-start(s32[256]{0:T(256)} %param.7) | copy-start | bytes 3076
  305.7 1.9 copy-start.3
  305.8 1.9 copy-start.2
  309.7 216.2 %all-reduce.3.cloned.1.call-start = ((), (), s32[]{:S(2)}) async-start(), calls=%async_computation.3 | async-start | bytes 294912
Sparse Core Ops, SparseCore 0:
  63.1 43.1 all-gather.1
  309.8 60.2 reduce-scatter.2
  373.6 152.2 all-reduce.2
where the time goes:
time: 534 us
  waiting for transfers between devices  254 us (48%)
  blocking collectives  244 us (46%)
  between operations  14.5 us (3%)
  matrix products  13.5 us (3%)
    unnamed x4, waiting for transfers between devices  153 us
    psum x1, blocking collectives, local(): row_total = lax.psum(jnp.sum(exponent, axis=1), ('tok', 'voc'))  96.8 us
    psum x1, blocking collectives, local(): lax.psum(jnp.sum(probability * cap_tangent, axis=1), ('tok', 'voc'))  94.9 us
    reduce_scatter x1, waiting for transfers between devices, local(): lax.psum_scatter(probe_part + head_part, 'tok', scatter_dimension=0, tile...  58.5 us
    all_gather x1, blocking collectives, local(): features = lax.all_gather(stacked, 'voc', axis=2, tiled=True)  52.7 us
    all_gather x1, waiting for transfers between devices, local(): gathered = lax.all_gather(features, 'tok', axis=1, tiled=True)  42.7 us
  transfers between devices with their start and end apart: 3, of which 3 were waited for; matrix products, arithmetic and copies ran while one was open for 1% of the time, Pallas kernels for 0%

commit v1 on v0

--- a/solution.py
+++ b/solution.py
@@ -23,7 +23,9 @@
     cap_slope = 1.0 - capped * capped
     exponent = jnp.exp(softcap_value * capped)
     cap_tangent = cap_slope * tangent
-    row_total = lax.psum(jnp.sum(exponent, axis=1), ("tok", "voc"))
+    own = jnp.sum(exponent, axis=1)
+    parts = lax.all_gather(own, ("tok", "voc"))
+    row_total = jnp.sum(parts, axis=0)
     probability = exponent / row_total[:, None]
     mean_tangent = lax.psum(jnp.sum(probability * cap_tangent, axis=1), ("tok", "voc"))
     factor = 1.0 + 2.0 * zloss_weight * jnp.log(row_total)

time: 534 us -> 558 us (1.045)
  blocking collectives: 244 us -> 267 us
    all_gather x0 -> x1, blocking collectives: none -> 118 us  [local(): parts = lax.all_gather(own, ('tok', 'voc'))]
    psum x1 -> x0, blocking collectives: 96.8 us -> none  [local(): row_total = lax.psum(jnp.sum(exponent, axis=1), ('tok', 'voc'))]
where the time goes in v1:
time: 558 us
  blocking collectives  267 us (48%)
  waiting for transfers between devices  254 us (46%)
  between operations  14.5 us (3%)
  matrix products  13.5 us (2%)
    unnamed x4, waiting for transfers between devices  153 us
    all_gather x1, blocking collectives, local(): parts = lax.all_gather(own, ('tok', 'voc'))  118 us
    psum x1, blocking collectives, local(): lax.psum(jnp.sum(probability * cap_tangent, axis=1), ('tok', 'voc'))  96.4 us
    reduce_scatter x1, waiting for transfers between devices, local(): lax.psum_scatter(probe_part + head_part, 'tok', scatter_dimension=0, tile...  58.5 us
    all_gather x1, blocking collectives, local(): features = lax.all_gather(stacked, 'voc', axis=2, tiled=True)  52.7 us
    all_gather x1, waiting for transfers between devices, local(): gathered = lax.all_gather(features, 'tok', axis=1, tiled=True)  42.7 us
  transfers between devices with their start and end apart: 3, of which 3 were waited for; matrix products, arithmetic and copies ran while one was open for 1% of the time, Pallas kernels for 0%

profile of v1, /device:TPU:2, one launch (start us, length us, event | category | flops | bytes accessed | tf_op | source)
XLA Modules:
  0.0 557.9 jit_solution(14523745523806159616)
XLA Ops:
  7.2 0.0 copy-start
  7.2 0.0 all-gather.4.cloned.1.call-start
  7.2 0.8 pad_maximum_fusion
  8.0 0.1 copy.12
  8.1 52.7 %all_gather.12 = bf16[2,16,2304]{1,0,2:T(2,128)(2,1)S(1)} all-gather(bf16[2,16,72]{1,0,2:T(2,128)(2,1)S(1)} %copy.12), channel_id=1, replica_groups=mesh['tok'=16,'voc'=32] {'voc'}, dimensions={2}, use_global_device_ids=true | all-gather | bytes 152064 | tf_op jit(solution)/shard_map/all_gather | solution.py:14
  60.8 2.2 copy.13
  63.0 0.0 all-gather.4.cloned.1.call-update
  63.0 0.0 reduce-scatter.3.cloned.1.call-start
  63.1 0.6 iota_add_fusion
  63.7 42.7 %all-gather.4.cloned.1.call-done = bf16[2,256,2304]{2,1,0:T(8,128)(2,1)} async-done(((bf16[2,16,2304]{2,1,0:T(8,128)(2,1)}), bf16[2,256,2304]{2,1,0:T(8,128)(2,1)}) %all-gather.4.cloned.1.call-update) | async-done | bytes 2359312 | tf_op jit(solution)/shard_map/all_gather | solution.py:15
  106.4 0.0 copy-done
  106.4 2.7 fusion.8
  109.1 117.8 %all-gather.1 = f32[512,1,256]{2,1,0:T(1,128)} all-gather(f32[1,1,256]{2,1,0:T(1,128)S(1)} %bitcast.35), channel_id=2, replica_groups=mesh['tok'=16,'voc'=32] {'tok','voc'}, dimensions={0}, use_global_device_ids=true | all-gather | bytes 525312 | tf_op jit(solution)/shard_map/all_gather | solution.py:27
  226.8 1.6 reduce_sum.28
  228.4 0.0 copy-done.1
  228.4 0.0 copy-start.4
  228.4 1.9 fusion.3
  230.4 0.0 copy-done.4
  230.4 0.0 copy-start.5
  230.4 1.8 multiply_reduce_fusion
  232.2 96.4 %psum.7 = f32[256]{0:T(256)S(1)} all-reduce(f32[256]{0:T(256)} %get-tuple-element.6), channel_id=1, replica_groups=mesh['tok'=16,'voc'=32] {'tok','voc'}, use_global_device_ids=true, to_apply=%region_3.0 | all-reduce | flops 256 | bytes 2048 | tf_op jit(solution)/shard_map/psum | solution.py:30
  328.6 1.2 add_convert_fusion
  329.8 1.9 fusion.10
  331.8 2.0 convolution_add_fusion
  333.7 0.0 reduce-scatter.3.cloned.1.call-update
  333.7 0.0 all-reduce.3.cloned.1.call-start
  333.8 1.3 dynamic-slice
  335.7 58.5 %reduce-scatter.3.cloned.1.call-done = f32[16,2304]{1,0:T(8,128)} async-done(((f32[256,2304]{1,0:T(8,128)}), f32[16,2304]{1,0:T(8,128)}) %reduce-scatter.3.cloned.1.call-update) | async-done | bytes 147472 | tf_op jit(solution)/shard_map/reduce_scatter | solution.py:52
  394.2 0.0 all-reduce.3.cloned.1.call-update
  394.2 3.2 convolution_bitcast_fusion
  397.4 152.5 %all-reduce.3.cloned.1.call-done = f32[16,2304]{1,0:T(8,128)} async-done(((f32[16,2304]{1,0:T(8,128)}), f32[16,2304]{1,0:T(8,128)}) %all-reduce.3.cloned.1.call-update) | async-done | bytes 147472
  550.0 1.4 constant_dynamic-slice_fusion
  (8 shorter events, 0.0 us)
Async XLA Ops:
  7.2 99.2 %copy-start = (bf16[2304,256]{1,0:T(8,128)(2,1)S(1)}, bf16[2304,256]{1,0:T(8,128)(2,1)}, u32[]{:S(2)}) copy-start(bf16[2304,256]{1,0:T(8,128)(2,1)} %param.6) | copy-start | bytes 3538948
  7.2 99.2 %all-gather.4.cloned.1.call-start = ((), (), s32[]{:S(2)}) async-start(), calls=%async_computation.1 | async-start | bytes 2506752 | tf_op jit(solution)/shard_map/all_gather | solution.py:15
  63.0 331.2 %reduce-scatter.3.cloned.1.call-start = ((), (), s32[]{:S(2)}) async-start(), calls=%async_computation.2 | async-start | bytes 2506752 | tf_op jit(solution)/shard_map/reduce_scatter | solution.py:52
  106.4 122.1 %copy-start.1 = (bf16[2,256,2304]{2,1,0:T(8,128)(2,1)S(1)}, bf16[2,256,2304]{2,1,0:T(8,128)(2,1)}, u32[]{:S(2)}) copy-start(bf16[2,256,2304]{2,1,0:T(8,128)(2,1)} %all-gather.4.cloned.1.call-done) | copy-start | bytes 7077892
  228.4 1.9 copy-start.4
  230.4 98.2 %copy-start.5 = (s32[256]{0:T(256)S(1)}, s32[256]{0:T(256)}, u32[]{:S(2)}) copy-start(s32[256]{0:T(256)} %param.7) | copy-start | bytes 3076
  329.8 1.9 copy-start.3
  329.8 1.9 copy-start.2
  333.7 216.2 %all-reduce.3.cloned.1.call-start = ((), (), s32[]{:S(2)}) async-start(), calls=%async_computation.3 | async-start | bytes 294912
Sparse Core Ops, SparseCore 0:
  63.1 43.1 all-gather.3
  333.9 60.2 reduce-scatter.2
  397.7 152.2 all-reduce.2
